TPU v7x, 32 devices: a whole 2x2x4 slice. The times are simulated.
32 devices in a mesh: seq: 8 (over z, core), tp: 4 (over y, x).
Axes of the slice: x: 2, y: 2, z: 4, core: 2. Of those that a mesh axis runs over, the one named last changes fastest.
Arguments:
- tokens: bfloat16 [64, 6144], P('seq'), may hold values from -6 to 6
- out_grad: bfloat16 [64, 6144], P('seq'), may hold values from -1.5 to 1.5
- w_in: bfloat16 [6144, 24576], P('seq', 'tp'), may hold values from -0.078125 to 0.078125
- w_out: bfloat16 [24576, 6144], P('tp', 'seq'), may hold values from -0.0390625 to 0.0390625
Outputs:
- input_grad: bfloat16 [64, 6144], P('tp', 'seq')
- grad_in: float32 [6144, 24576], P('seq', 'tp')
- grad_out: float32 [24576, 6144], P('tp', 'seq')
All inputs are finite; a program needn't handle non-finite values.
Results may differ from a plain program's by a relative error of at most 0.0051.
Values may be sent and summed in bfloat16 or wider, within the bound.
A program may use at most 128 MiB of HBM per device.

v0:
```python
import jax
import jax.numpy as jnp
from jax import lax
from jax.sharding import PartitionSpec as P


def over_rows(left, right):
    return lax.dot_general(
        left, right, (((0,), (0,)), ((), ())), preferred_element_type=jnp.float32
    )


def over_cols(left, right):
    return lax.dot_general(
        left, right, (((1,), (1,)), ((), ())), preferred_element_type=jnp.float32
    )


def per_device(tokens, out_grad, w_in, w_out):
    cols_x, cols_dy = (
        lax.all_to_all(tokens, "seq", split_axis=1, concat_axis=0, tiled=True),
        lax.all_to_all(out_grad, "seq", split_axis=1, concat_axis=0, tiled=True),
    )
    pre = jnp.dot(cols_x, w_in, preferred_element_type=jnp.float32)
    hidden_grad = over_cols(cols_dy, w_out)
    pre_share, grad_share = (
        lax.psum_scatter(pre, "seq", scatter_dimension=0, tiled=True),
        lax.psum_scatter(hidden_grad, "seq", scatter_dimension=0, tiled=True),
    )
    posit = jnp.maximum(pre_share, 0.0)
    act = (posit * posit).astype(jnp.bfloat16)
    slope = (2.0 * posit * grad_share).astype(jnp.bfloat16)
    act_piece = lax.all_gather(act, "seq", axis=0, tiled=True)
    slope_piece = lax.all_gather(slope, "seq", axis=0, tiled=True)
    sum_out = over_rows(act_piece, cols_dy)
    sum_in = over_rows(cols_x, slope_piece)
    partial_value = over_cols(slope_piece, w_in)
    grad_in, grad_out, partial_value = (sum_in, sum_out, partial_value)
    input_grad = lax.psum_scatter(partial_value, "tp", scatter_dimension=0, tiled=True).astype(
        jnp.bfloat16
    )
    return (input_grad, grad_in, grad_out)


def solution(mesh):
    return jax.shard_map(
        per_device,
        mesh=mesh,
        in_specs=(P("seq", None), P("seq", None), P("seq", "tp"), P("tp", "seq")),
        out_specs=(P("tp", "seq"), P("seq", "tp"), P("tp", "seq")),
        check_vma=False,
    )
```

profile of v0, /device:TPU:0, one launch (start us, length us, event | category | flops | bytes accessed | tf_op | source)
XLA Modules:
  0.0 180.2 jit_solution(3376550464443689663)
XLA Ops:
  7.2 0.0 reduce-scatter.6.cloned.1.call-start
  7.2 12.7 %all_to_all.38 = bf16[8,8,768]{2,0,1:T(8,128)(2,1)S(1)} all-to-all(bf16[8,8,768]{2,0,1:T(8,128)(2,1)} %bitcast.24), channel_id=1, replica_groups=mesh['seq'=8,'tp'=4] {'seq'}, dimensions={1} | all-to-all | bytes 196608 | tf_op jit(solution)/shard_map/all_to_all | solution.py:22
  19.9 0.0 copy-start
  19.9 7.8 %fusion.2 = f32[64,6144]{1,0:T(8,128)} fusion(bf16[6144,768]{1,0:T(8,128)(2,1)} %param.7, bf16[8,8,768]{2,0,1:T(8,128)(2,1)S(1)} %all_to_all.38), kind=kOutput, calls=%fused_computation.5 | convolution fusion | flops 603979776 | bytes 11108352 | tf_op jit(solution)/shard_map/dot_general | solution.py:14
  27.7 0.0 reduce-scatter.6.cloned.1.call-update
  27.7 0.0 reduce-scatter.4.cloned.1.call-start
  27.8 0.0 copy-done
  27.8 8.8 %all_to_all.39 = bf16[8,8,768]{2,0,1:T(8,128)(2,1)S(1)} all-to-all(bf16[8,8,768]{2,0,1:T(8,128)(2,1)S(1)} %bitcast.25), channel_id=1, replica_groups=mesh['seq'=8,'tp'=4] {'seq'}, dimensions={1} | all-to-all | bytes 196608 | tf_op jit(solution)/shard_map/all_to_all | solution.py:21
  36.6 6.6 %fusion.5 = f32[64,6144]{1,0:T(8,128)} fusion(bf16[768,6144]{1,0:T(8,128)(2,1)} %param.6, bf16[8,8,768]{2,0,1:T(8,128)(2,1)S(1)} %all_to_all.39), kind=kOutput, calls=%fused_computation.8 | convolution fusion | flops 603979776 | bytes 11108352 | tf_op jit(solution)/shard_map/dot_general | solution.py:24
  43.2 0.0 reduce-scatter.4.cloned.1.call-update
  43.2 0.0 reduce-scatter.8.cloned.1.call-start
  43.3 17.8 %reduce-scatter.6.cloned.1.call-done = f32[8,6144]{1,0:T(8,128)} async-done(((f32[64,6144]{1,0:T(8,128)}), f32[8,6144]{1,0:T(8,128)}) %reduce-scatter.6.cloned.1.call-update) | async-done | bytes 196624 | tf_op jit(solution)/shard_map/reduce_scatter | solution.py:28
  61.0 35.5 %reduce-scatter.4.cloned.1.call-done = f32[8,6144]{1,0:T(8,128)} async-done(((f32[64,6144]{1,0:T(8,128)}), f32[8,6144]{1,0:T(8,128)}) %reduce-scatter.4.cloned.1.call-update) | async-done | bytes 196624 | tf_op jit(solution)/shard_map/reduce_scatter | solution.py:27
  96.6 1.1 multiply_convert_fusion
  97.6 15.8 %all_gather.7 = bf16[64,6144]{1,0:T(8,128)(2,1)S(1)} all-gather(bf16[8,6144]{1,0:T(8,128)(2,1)S(1)} %get-tuple-element.6), channel_id=1, replica_groups=mesh['seq'=8,'tp'=4] {'seq'}, dimensions={0}, use_global_device_ids=true | all-gather | bytes 884736 | tf_op jit(solution)/shard_map/all_gather | solution.py:33
  113.4 16.2 %all_gather.6 = bf16[64,6144]{1,0:T(8,128)(2,1)S(1)} all-gather(bf16[8,6144]{1,0:T(8,128)(2,1)S(1)} %get-tuple-element.7), channel_id=1, replica_groups=mesh['seq'=8,'tp'=4] {'seq'}, dimensions={0}, use_global_device_ids=true | all-gather | bytes 884736 | tf_op jit(solution)/shard_map/all_gather | solution.py:34
  129.6 7.3 %fusion.7 = f32[64,768]{1,0:T(8,128)} fusion(bf16[64,6144]{1,0:T(8,128)(2,1)S(1)} %all_gather.6, bf16[768,6144]{1,0:T(8,128)(2,1)} %param.6), kind=kOutput, calls=%fused_computation.10 | convolution fusion | flops 603979776 | bytes 10420224 | tf_op jit(solution)/shard_map/dot_general | solution.py:14
  136.9 0.0 reduce-scatter.8.cloned.1.call-update
  137.0 8.3 %convolution_bitcast_fusion = f32[768,6144]{0,1:T(8,128)} fusion(bf16[64,6144]{1,0:T(8,128)(2,1)S(1)} %all_gather.6, bf16[8,8,768]{2,0,1:T(8,128)(2,1)S(1)} %all_to_all.39), kind=kOutput, calls=%fused_computation | convolution fusion | flops 603979776 | bytes 19759104 | tf_op jit(solution)/shard_map/dot_general | solution.py:8
  145.3 18.7 %copy.7 = f32[768,6144]{1,0:T(8,128)} copy(f32[768,6144]{0,1:T(8,128)} %convolution_bitcast_fusion) | data formatting | bytes 37748736
  164.0 8.3 %fusion = f32[6144,768]{1,0:T(8,128)} fusion(bf16[64,6144]{1,0:T(8,128)(2,1)S(1)} %all_gather.7, bf16[8,8,768]{2,0,1:T(8,128)(2,1)S(1)} %all_to_all.38), kind=kOutput, calls=%fused_computation.3 | convolution fusion | flops 603979776 | bytes 19759104 | tf_op jit(solution)/shard_map/dot_general | solution.py:8
  172.2 0.0 reduce-scatter.8.cloned.1.call-done
  172.2 1.4 convert_element_type.10
Async XLA Ops:
  7.2 53.9 %reduce-scatter.6.cloned.1.call-start = ((), (), s32[]{:S(2)}) async-start(), calls=%async_computation.6 | async-start | bytes 1769472 | tf_op jit(solution)/shard_map/reduce_scatter | solution.py:28
  19.9 7.9 %copy-start = (bf16[8,6144]{1,0:T(8,128)(2,1)S(1)}, bf16[8,6144]{1,0:T(8,128)(2,1)}, u32[]{:S(2)}) copy-start(bf16[8,6144]{1,0:T(8,128)(2,1)} %param.4) | copy-start | bytes 294916
  27.7 68.9 %reduce-scatter.4.cloned.1.call-start = ((), (), s32[]{:S(2)}) async-start(), calls=%async_computation.5 | async-start | bytes 1769472 | tf_op jit(solution)/shard_map/reduce_scatter | solution.py:27
  43.2 129.0 %reduce-scatter.8.cloned.1.call-start = ((), (), s32[]{:S(2)}) async-start(), calls=%async_computation.7 | async-start | bytes 245760 | tf_op jit(solution)/shard_map/reduce_scatter | solution.py:39
Sparse Core Ops, SparseCore 0:
  27.8 33.1 reduce-scatter.5
  63.9 32.6 reduce-scatter.3
  137.1 21.8 reduce-scatter.7
where the time goes:
time: 181 us; the launch traced here: 180 us
  blocking collectives  53.5 us (30%)
  waiting for transfers between devices  53.3 us (29%)
  matrix products  38.3 us (21%)
  local copies, waits for them, and re-layouts  18.7 us (10%)
  between operations  13.8 us (8%)
  other arithmetic  2.47 us (1%)
    reduce_scatter x1, waiting for transfers between devices, per_device(): lax.psum_scatter(pre, 'seq', scatter_dimension=0, tiled=True)  35.5 us
    unnamed x3, local copies, waits for them, and re-layouts  18.7 us
    reduce_scatter x1, waiting for transfers between devices, per_device(): lax.psum_scatter(hidden_grad, 'seq', scatter_dimension=0, tiled=True)  17.8 us
    dot_general x2, matrix products, over_rows(): lax.dot_general(left, right, (((0,), (0,)), ((), ())), preferred_element_...  16.6 us
    all_gather x1, blocking collectives, per_device(): slope_piece = lax.all_gather(slope, 'seq', axis=0, tiled=True)  16.2 us
    all_gather x1, blocking collectives, per_device(): act_piece = lax.all_gather(act, 'seq', axis=0, tiled=True)  15.8 us
    dot_general x2, matrix products, over_cols(): lax.dot_general(left, right, (((1,), (1,)), ((), ())), preferred_element_...  15.1 us
    all_to_all x1, blocking collectives, per_device(): lax.all_to_all(out_grad, 'seq', split_axis=1, concat_axis=0, tiled=True)  12.7 us
  transfers between devices with their start and end apart: 3, of which 2 were waited for; matrix products, arithmetic and copies ran while one was open for 23% of the time, Pallas kernels for 0%

commit v1 on v0

--- a/solution.py
+++ b/solution.py
@@ -30,8 +30,10 @@
     posit = jnp.maximum(pre_share, 0.0)
     act = (posit * posit).astype(jnp.bfloat16)
     slope = (2.0 * posit * grad_share).astype(jnp.bfloat16)
-    act_piece = lax.all_gather(act, "seq", axis=0, tiled=True)
-    slope_piece = lax.all_gather(slope, "seq", axis=0, tiled=True)
+    n_now = jnp.concatenate([act, slope], 1)
+    act_piece, slope_piece = jnp.split(
+        lax.all_gather(n_now, "seq", axis=0, tiled=True), [act.shape[1]], 1
+    )
     sum_out = over_rows(act_piece, cols_dy)
     sum_in = over_rows(cols_x, slope_piece)
     partial_value = over_cols(slope_piece, w_in)

time: 181 us -> 173 us (0.956)
  blocking collectives: 53.5 us -> 21.5 us
  waiting for transfers between devices: 53.3 us -> 76.8 us
    all_gather x2 -> x0, blocking collectives: 32 us -> none  [the longest x1 16.2 us: per_device(): slope_piece = lax.all_gather(slope, 'seq', axis=0, tiled=True)]
    all_gather x0 -> x1, waiting for transfers between devices: none -> 23.4 us  [per_device(): lax.all_gather(n_now, 'seq', axis=0, tiled=True)]
    unnamed x3 -> x5, local copies, waits for them, and re-layouts: 18.7 us -> 18.7 us
  transfers between devices with their start and end apart: 3 -> 4, of which waited for: 2 -> 3; matrix products, arithmetic and copies ran while one was open for 23% -> 24% of each run, Pallas kernels for 0% -> 0%
where the time goes in v1:
time: 173 us
  waiting for transfers between devices  76.8 us (44%)
  matrix products  38.7 us (22%)
  blocking collectives  21.5 us (12%)
  local copies, waits for them, and re-layouts  18.7 us (11%)
  between operations  13.8 us (8%)
  other arithmetic  3.16 us (2%)
    reduce_scatter x1, waiting for transfers between devices, per_device(): lax.psum_scatter(pre, 'seq', scatter_dimension=0, tiled=True)  35.5 us
    all_gather x1, waiting for transfers between devices, per_device(): lax.all_gather(n_now, 'seq', axis=0, tiled=True)  23.4 us
    unnamed x5, local copies, waits for them, and re-layouts  18.7 us
    reduce_scatter x1, waiting for transfers between devices, per_device(): lax.psum_scatter(hidden_grad, 'seq', scatter_dimension=0, tiled=True)  17.8 us
    dot_general x2, matrix products, over_rows(): lax.dot_general(left, right, (((0,), (0,)), ((), ())), preferred_element_...  16.6 us
    dot_general x2, matrix products, over_cols(): lax.dot_general(left, right, (((1,), (1,)), ((), ())), preferred_element_...  15.5 us
    all_to_all x1, blocking collectives, per_device(): lax.all_to_all(out_grad, 'seq', split_axis=1, concat_axis=0, tiled=True)  12.7 us
    all_to_all x1, blocking collectives, per_device(): lax.all_to_all(tokens, 'seq', split_axis=1, concat_axis=0, tiled=True)  8.8 us
  transfers between devices with their start and end apart: 4, of which 3 were waited for; matrix products, arithmetic and copies ran while one was open for 24% of the time, Pallas kernels for 0%

profile of v1, /device:TPU:0, one launch (start us, length us, event | category | flops | bytes accessed | tf_op | source)
XLA Modules:
  0.0 172.8 jit_solution(10606730454432628950)
XLA Ops:
  7.2 0.0 reduce-scatter.6.cloned.1.call-start
  7.2 12.7 %all_to_all.38 = bf16[8,8,768]{2,0,1:T(8,128)(2,1)S(1)} all-to-all(bf16[8,8,768]{2,0,1:T(8,128)(2,1)} %bitcast.21), channel_id=1, replica_groups=mesh['seq'=8,'tp'=4] {'seq'}, dimensions={1} | all-to-all | bytes 196608 | tf_op jit(solution)/shard_map/all_to_all | solution.py:22
  19.9 0.0 copy-start.1
  19.9 7.8 %fusion.6 = f32[64,6144]{1,0:T(8,128)} fusion(bf16[6144,768]{1,0:T(8,128)(2,1)} %param.7, bf16[8,8,768]{2,0,1:T(8,128)(2,1)S(1)} %all_to_all.38), kind=kOutput, calls=%fused_computation.10 | convolution fusion | flops 603979776 | bytes 11108352 | tf_op jit(solution)/shard_map/dot_general | solution.py:14
  27.7 0.0 reduce-scatter.6.cloned.1.call-update
  27.7 0.0 reduce-scatter.4.cloned.1.call-start
  27.8 0.0 copy-done.1
  27.8 8.8 %all_to_all.39 = bf16[8,8,768]{2,0,1:T(8,128)(2,1)S(1)} all-to-all(bf16[8,8,768]{2,0,1:T(8,128)(2,1)S(1)} %bitcast.22), channel_id=1, replica_groups=mesh['seq'=8,'tp'=4] {'seq'}, dimensions={1} | all-to-all | bytes 196608 | tf_op jit(solution)/shard_map/all_to_all | solution.py:21
  36.6 6.6 %fusion.9 = f32[64,6144]{1,0:T(8,128)} fusion(bf16[768,6144]{1,0:T(8,128)(2,1)} %param.6, bf16[8,8,768]{2,0,1:T(8,128)(2,1)S(1)} %all_to_all.39), kind=kOutput, calls=%fused_computation.13 | convolution fusion | flops 603979776 | bytes 11108352 | tf_op jit(solution)/shard_map/dot_general | solution.py:24
  43.2 0.0 reduce-scatter.4.cloned.1.call-update
  43.2 0.0 all-gather.2.cloned.1.call-start
  43.3 17.8 %reduce-scatter.6.cloned.1.call-done = f32[8,6144]{1,0:T(8,128)} async-done(((f32[64,6144]{1,0:T(8,128)}), f32[8,6144]{1,0:T(8,128)}) %reduce-scatter.6.cloned.1.call-update) | async-done | bytes 196624 | tf_op jit(solution)/shard_map/reduce_scatter | solution.py:28
  61.0 35.5 %reduce-scatter.4.cloned.1.call-done = f32[8,6144]{1,0:T(8,128)} async-done(((f32[64,6144]{1,0:T(8,128)}), f32[8,6144]{1,0:T(8,128)}) %reduce-scatter.4.cloned.1.call-update) | async-done | bytes 196624 | tf_op jit(solution)/shard_map/reduce_scatter | solution.py:27
  96.6 1.1 multiply_convert_fusion.1
  97.6 0.7 pad_maximum_fusion
  98.3 0.0 all-gather.2.cloned.1.call-update
  98.3 0.0 reduce-scatter.8.cloned.1.call-start
  98.4 23.4 %all-gather.2.cloned.1.call-done = bf16[64,12288]{1,0:T(8,128)(2,1)} async-done(((bf16[8,12288]{1,0:T(8,128)(2,1)}), bf16[64,12288]{1,0:T(8,128)(2,1)}) %all-gather.2.cloned.1.call-update) | async-done | bytes 1572880 | tf_op jit(solution)/shard_map/all_gather | solution.py:35
  121.8 0.0 copy-start
  121.8 7.7 %fusion.3 = f32[64,768]{1,0:T(8,128)} fusion(bf16[768,6144]{1,0:T(8,128)(2,1)} %param.6, bf16[64,12288]{1,0:T(8,128)(2,1)} %all-gather.2.cloned.1.call-done), kind=kOutput, calls=%fused_computation.4 | convolution fusion | flops 603979776 | bytes 10420224 | tf_op jit(solution)/shard_map/dot_general | solution.py:14
  129.5 0.0 reduce-scatter.8.cloned.1.call-update
  129.6 0.0 copy-done
  129.6 8.3 %convolution_bitcast_fusion = f32[768,6144]{0,1:T(8,128)} fusion(bf16[64,12288]{1,0:T(8,128)(2,1)S(1)} %copy-done, bf16[8,8,768]{2,0,1:T(8,128)(2,1)S(1)} %all_to_all.39), kind=kOutput, calls=%fused_computation | convolution fusion | flops 603979776 | bytes 19759104 | tf_op jit(solution)/shard_map/dot_general | solution.py:8
  137.9 18.7 %copy.7 = f32[768,6144]{1,0:T(8,128)} copy(f32[768,6144]{0,1:T(8,128)} %convolution_bitcast_fusion) | data formatting | bytes 37748736
  156.5 8.3 %fusion = f32[6144,768]{1,0:T(8,128)} fusion(bf16[64,12288]{1,0:T(8,128)(2,1)S(1)} %copy-done, bf16[8,8,768]{2,0,1:T(8,128)(2,1)S(1)} %all_to_all.38), kind=kOutput, calls=%fused_computation.1 | convolution fusion | flops 603979776 | bytes 19759104 | tf_op jit(solution)/shard_map/dot_general | solution.py:8
  164.8 0.0 reduce-scatter.8.cloned.1.call-done
  164.8 1.4 convert_element_type.11
Async XLA Ops:
  7.2 53.9 %reduce-scatter.6.cloned.1.call-start = ((), (), s32[]{:S(2)}) async-start(), calls=%async_computation.6 | async-start | bytes 1769472 | tf_op jit(solution)/shard_map/reduce_scatter | solution.py:28
  19.9 7.9 %copy-start.1 = (bf16[8,6144]{1,0:T(8,128)(2,1)S(1)}, bf16[8,6144]{1,0:T(8,128)(2,1)}, u32[]{:S(2)}) copy-start(bf16[8,6144]{1,0:T(8,128)(2,1)} %param.4) | copy-start | bytes 294916
  27.7 68.9 %reduce-scatter.4.cloned.1.call-start = ((), (), s32[]{:S(2)}) async-start(), calls=%async_computation.5 | async-start | bytes 1769472 | tf_op jit(solution)/shard_map/reduce_scatter | solution.py:27
  43.2 78.6 %all-gather.2.cloned.1.call-start = ((), (), s32[]{:S(2)}) async-start(), calls=%async_computation.7 | async-start | bytes 1769472 | tf_op jit(solution)/shard_map/all_gather | solution.py:35
  98.3 66.5 %reduce-scatter.8.cloned.1.call-start = ((), (), s32[]{:S(2)}) async-start(), calls=%async_computation.8 | async-start | bytes 245760 | tf_op jit(solution)/shard_map/reduce_scatter | solution.py:41
  121.8 7.7 %copy-start = (bf16[64,12288]{1,0:T(8,128)(2,1)S(1)}, bf16[64,12288]{1,0:T(8,128)(2,1)}, u32[]{:S(2)}) copy-start(bf16[64,12288]{1,0:T(8,128)(2,1)} %all-gather.2.cloned.1.call-done) | copy-start | bytes 4718596
Sparse Core Ops, SparseCore 0:
  27.8 33.1 reduce-scatter.5
  63.9 32.6 reduce-scatter.3
  98.8 23.0 all-gather.1
  129.7 23.5 reduce-scatter.7

commit v2 on v0

--- a/solution.py
+++ b/solution.py
@@ -2,6 +2,15 @@
 import jax.numpy as jnp
 from jax import lax
 from jax.sharding import PartitionSpec as P
+
+
+def _guide_set(page, axis_no, where_dim):
+    reply = lax.axis_size("seq")
+    mat_out = jnp.split(page, reply, axis=axis_no)
+    state_now = jnp.stack(mat_out)
+    parts_out = lax.all_to_all(state_now, "seq", 0, 0)
+    current_arr = jnp.concatenate(parts_out, axis=where_dim)
+    return current_arr
 
 
 def over_rows(left, right):
@@ -19,7 +28,7 @@
 def per_device(tokens, out_grad, w_in, w_out):
     cols_x, cols_dy = (
         lax.all_to_all(tokens, "seq", split_axis=1, concat_axis=0, tiled=True),
-        lax.all_to_all(out_grad, "seq", split_axis=1, concat_axis=0, tiled=True),
+        _guide_set(out_grad, 1, where_dim=0),
     )
     pre = jnp.dot(cols_x, w_in, preferred_element_type=jnp.float32)
     hidden_grad = over_cols(cols_dy, w_out)

time: 181 us -> 186 us (1.028)
  local copies, waits for them, and re-layouts: 18.7 us -> 24.4 us
    unnamed x3 -> x10, local copies, waits for them, and re-layouts: 18.7 us -> 23.7 us
where the time goes in v2:
time: 186 us
  blocking collectives  53.2 us (29%)
  waiting for transfers between devices  53.2 us (29%)
  matrix products  38.3 us (21%)
  local copies, waits for them, and re-layouts  24.4 us (13%)
  between operations  13.8 us (7%)
  other arithmetic  2.47 us (1%)
    reduce_scatter x1, waiting for transfers between devices, per_device(): lax.psum_scatter(pre, 'seq', scatter_dimension=0, tiled=True)  35.4 us
    unnamed x10, local copies, waits for them, and re-layouts  23.7 us
    reduce_scatter x1, waiting for transfers between devices, per_device(): lax.psum_scatter(hidden_grad, 'seq', scatter_dimension=0, tiled=True)  17.7 us
    dot_general x2, matrix products, over_rows(): lax.dot_general(left, right, (((0,), (0,)), ((), ())), preferred_element_...  16.6 us
    all_gather x1, blocking collectives, per_device(): slope_piece = lax.all_gather(slope, 'seq', axis=0, tiled=True)  16.2 us
    all_gather x1, blocking collectives, per_device(): act_piece = lax.all_gather(act, 'seq', axis=0, tiled=True)  15.8 us
    dot_general x2, matrix products, over_cols(): lax.dot_general(left, right, (((1,), (1,)), ((), ())), preferred_element_...  15.1 us
    all_to_all x1, blocking collectives, _guide_set(): parts_out = lax.all_to_all(state_now, 'seq', 0, 0)  12.5 us
  transfers between devices with their start and end apart: 3, of which 2 were waited for; matrix products, arithmetic and copies ran while one was open for 23% of the time, Pallas kernels for 0%

profile of v2, /device:TPU:0, one launch (start us, length us, event | category | flops | bytes accessed | tf_op | source)
XLA Modules:
  0.0 185.5 jit_solution(11296879922567359979)
XLA Ops:
  7.2 0.0 reduce-scatter.6.cloned.1.call-start
  7.2 0.7 constant_dynamic-update-slice_fusion.7
  7.9 0.7 constant_dynamic-update-slice_fusion.6
  8.6 0.7 constant_dynamic-update-slice_fusion.5
  9.3 0.7 constant_dynamic-update-slice_fusion.4
  10.1 0.7 constant_dynamic-update-slice_fusion.3
  10.8 0.7 constant_dynamic-update-slice_fusion.2
  11.5 0.7 constant_dynamic-update-slice_fusion.1
  12.2 0.7 constant_dynamic-update-slice_fusion
  12.9 12.5 %all_to_all.24 = bf16[8,8,768]{2,1,0:T(8,128)(2,1)S(1)} all-to-all(bf16[8,8,768]{2,1,0:T(8,128)(2,1)S(1)} %constant_dynamic-update-slice_fusion), channel_id=1, replica_groups=mesh['seq'=8,'tp'=4] {'seq'}, dimensions={0} | all-to-all | bytes 196608 | tf_op jit(solution)/shard_map/all_to_all | solution.py:11
  25.4 0.0 copy-start
  25.4 7.8 %fusion.5 = f32[64,6144]{1,0:T(8,128)} fusion(bf16[6144,768]{1,0:T(8,128)(2,1)} %param.7, bf16[8,8,768]{2,1,0:T(8,128)(2,1)S(1)} %all_to_all.24), kind=kOutput, calls=%fused_computation.8 | convolution fusion | flops 603979776 | bytes 11108352 | tf_op jit(solution)/shard_map/dot_general | solution.py:23
  33.2 0.0 reduce-scatter.6.cloned.1.call-update
  33.2 0.0 reduce-scatter.4.cloned.1.call-start
  33.2 0.0 copy-done
  33.2 8.8 %all_to_all.25 = bf16[8,8,768]{2,0,1:T(8,128)(2,1)S(1)} all-to-all(bf16[8,8,768]{2,0,1:T(8,128)(2,1)S(1)} %bitcast.37), channel_id=1, replica_groups=mesh['seq'=8,'tp'=4] {'seq'}, dimensions={1} | all-to-all | bytes 196608 | tf_op jit(solution)/shard_map/all_to_all | solution.py:30
  42.0 6.6 %fusion.1 = f32[64,6144]{1,0:T(8,128)} fusion(bf16[768,6144]{1,0:T(8,128)(2,1)} %param.6, bf16[8,8,768]{2,0,1:T(8,128)(2,1)S(1)} %all_to_all.25), kind=kOutput, calls=%fused_computation.4 | convolution fusion | flops 603979776 | bytes 11108352 | tf_op jit(solution)/shard_map/dot_general | solution.py:33
  48.7 0.0 reduce-scatter.4.cloned.1.call-update
  48.7 0.0 reduce-scatter.8.cloned.1.call-start
  48.8 17.7 %reduce-scatter.6.cloned.1.call-done = f32[8,6144]{1,0:T(8,128)} async-done(((f32[64,6144]{1,0:T(8,128)}), f32[8,6144]{1,0:T(8,128)}) %reduce-scatter.6.cloned.1.call-update) | async-done | bytes 196624 | tf_op jit(solution)/shard_map/reduce_scatter | solution.py:37
  66.5 35.4 %reduce-scatter.4.cloned.1.call-done = f32[8,6144]{1,0:T(8,128)} async-done(((f32[64,6144]{1,0:T(8,128)}), f32[8,6144]{1,0:T(8,128)}) %reduce-scatter.4.cloned.1.call-update) | async-done | bytes 196624 | tf_op jit(solution)/shard_map/reduce_scatter | solution.py:36
  101.9 1.1 multiply_convert_fusion
  103.0 15.8 %all_gather.7 = bf16[64,6144]{1,0:T(8,128)(2,1)S(1)} all-gather(bf16[8,6144]{1,0:T(8,128)(2,1)S(1)} %get-tuple-element.6), channel_id=1, replica_groups=mesh['seq'=8,'tp'=4] {'seq'}, dimensions={0}, use_global_device_ids=true | all-gather | bytes 884736 | tf_op jit(solution)/shard_map/all_gather | solution.py:42
  118.8 16.2 %all_gather.6 = bf16[64,6144]{1,0:T(8,128)(2,1)S(1)} all-gather(bf16[8,6144]{1,0:T(8,128)(2,1)S(1)} %get-tuple-element.7), channel_id=1, replica_groups=mesh['seq'=8,'tp'=4] {'seq'}, dimensions={0}, use_global_device_ids=true | all-gather | bytes 884736 | tf_op jit(solution)/shard_map/all_gather | solution.py:43
  135.0 7.3 %fusion.7 = f32[64,768]{1,0:T(8,128)} fusion(bf16[64,6144]{1,0:T(8,128)(2,1)S(1)} %all_gather.6, bf16[768,6144]{1,0:T(8,128)(2,1)} %param.6), kind=kOutput, calls=%fused_computation.18 | convolution fusion | flops 603979776 | bytes 10420224 | tf_op jit(solution)/shard_map/dot_general | solution.py:23
  142.3 0.0 reduce-scatter.8.cloned.1.call-update
  142.3 8.3 %convolution_bitcast_fusion = f32[768,6144]{0,1:T(8,128)} fusion(bf16[64,6144]{1,0:T(8,128)(2,1)S(1)} %all_gather.6, bf16[8,8,768]{2,0,1:T(8,128)(2,1)S(1)} %all_to_all.25), kind=kOutput, calls=%fused_computation | convolution fusion | flops 603979776 | bytes 19759104 | tf_op jit(solution)/shard_map/dot_general | solution.py:17
  150.6 18.7 %copy.7 = f32[768,6144]{1,0:T(8,128)} copy(f32[768,6144]{0,1:T(8,128)} %convolution_bitcast_fusion) | data formatting | bytes 37748736
  169.3 8.3 %fusion.3 = f32[6144,768]{1,0:T(8,128)} fusion(bf16[64,6144]{1,0:T(8,128)(2,1)S(1)} %all_gather.7, bf16[8,8,768]{2,1,0:T(8,128)(2,1)S(1)} %all_to_all.24), kind=kOutput, calls=%fused_computation.6 | convolution fusion | flops 603979776 | bytes 19759104 | tf_op jit(solution)/shard_map/dot_general | solution.py:17
  177.6 0.0 reduce-scatter.8.cloned.1.call-done
  177.6 1.4 convert_element_type.10
Async XLA Ops:
  7.2 59.3 %reduce-scatter.6.cloned.1.call-start = ((), (), s32[]{:S(2)}) async-start(), calls=%async_computation.6 | async-start | bytes 1769472 | tf_op jit(solution)/shard_map/reduce_scatter | solution.py:37
  25.4 7.9 %copy-start = (bf16[8,6144]{1,0:T(8,128)(2,1)S(1)}, bf16[8,6144]{1,0:T(8,128)(2,1)}, u32[]{:S(2)}) copy-start(bf16[8,6144]{1,0:T(8,128)(2,1)} %param.4) | copy-start | bytes 294916
  33.2 68.8 %reduce-scatter.4.cloned.1.call-start = ((), (), s32[]{:S(2)}) async-start(), calls=%async_computation.5 | async-start | bytes 1769472 | tf_op jit(solution)/shard_map/reduce_scatter | solution.py:36
  48.7 128.9 %reduce-scatter.8.cloned.1.call-start = ((), (), s32[]{:S(2)}) async-start(), calls=%async_computation.7 | async-start | bytes 245760 | tf_op jit(solution)/shard_map/reduce_scatter | solution.py:48
Sparse Core Ops, SparseCore 0:
  33.3 33.1 reduce-scatter.5
  69.4 32.5 reduce-scatter.3
  142.4 22.1 reduce-scatter.7
